TPU v7x, 256 devices: a whole 4x4x8 slice. The times are simulated.
256 devices in a mesh: row: 16 (over y, x), col: 16 (over z, core).
Axes of the slice: x: 4, y: 4, z: 8, core: 2. Of those that a mesh axis runs over, the one named last changes fastest.
Arguments:
- amplitudes: float32 [128, 128, 6144], P('col', 'row'), may hold values from -6 to 6
- integrals: float32 [6144, 6144], P('col', 'row'), may hold values from -0.078125 to 0.078125
- amp_pattern: int32 [128, 48], P('col'), may hold values 0 or 1
- int_pattern: int32 [48, 48], P(None, 'row'), may hold values from 0 to 1
Outputs:
- ladder: float32 [128, 128, 6144], P('col', 'row')
All inputs are finite; a program needn't handle non-finite values. No bound on the sum of `amp_pattern` on one device may be relied on, other than what follows from the above.
Results may differ from a plain program's by a relative error of at most 0.00007.
Values sent between devices are 32-bit elements; how exact they have to be, the bound alone decides.
A program may use at most 128 MiB of HBM per device.

v0:
```python
import jax
import jax.numpy as jnp
from jax import lax
from jax.experimental import pallas as pl
from jax.experimental.pallas import tpu as pltpu
from jax.sharding import PartitionSpec as P

TILE = 128
MESH = pl.DeviceIdType.MESH
RING, SZ = 4, 8
PARTS = 2
B1, B2, B3, XA, LA, XE, A1, A2 = range(8)
CUT = 32
FULL, WIDE, NARROW = (0, 384), (0, 256), (256, 128)
SPANS = (FULL, WIDE, NARROW)
UNITS = ((0, FULL), (1, FULL), (3, FULL), (2, WIDE), (2, NARROW))

PROGRAM = (
    (1153, 1793, 1157, 1797, 1664, 1668, 1029, 1037, 512, 1409, 1413, 528, 1425, 1429, 1025, 1672, 560, 1457, 1461,
     1161, 1165, 769, 1794, 520, 1417, 1421, 1925, 5, 1201, 1205, 385, 1410, 544, 1445, 129, 137, 1282, 1676, 1,
     1173, 1688, 401, 1426, 1169, 1692, 536, 1437, 1680, 393, 1418, 1933, 1684, 13, 1213, 773, 1949, 568, 1469,
     1033, 1209, 1433, 770, 1941, 1026, 552, 1453, 1465, 1290, 386, 389, 394, 397,),
    (),
    (433, 1458, 177, 185, 1330, 1921, 133, 141,),
    (409, 1434, 9, 1177, 1181, 258,),
    (266,),
    (441, 1466, 1441, 1034, 1338, 1929, 2, 1189, 1449, 897, 402, 405, 410, 413,),
    (901, 434, 437, 442, 445,),
    (417, 1442, 909,),
    (1185, 1922, 1945, 181, 189, 925,),
    (425, 1450, 10, 1193, 1197, 905, 1930, 145, 153,),
    (1937, 306, 917,),
    (921, 1946, 149, 157,),
    (913, 1938, 898, 418, 421, 426, 429,),
    (2048, 1298, 314,),
    (165, 173, 922,),
    (2064, 2176, 161, 169, 1314, 906,),
    (2056, 1306, 2184, 274,),
    (2192, 2304, 1322, 290, 914,),
    (2072, 2312, 282,),
    (2200, 298,),
    (2080, 2320, 2208, 2328, 2336,),
)
ORDER = ((0, 0, 0), (0, 1, 0), (0, 3, 0), (1, 2, 0), (2, 2, 0), (0, 0, 1), (0, 0, 3), (0, 1, 3), (0, 3, 3), (0, 1,
    1), (1, 2, 3), (0, 3, 1), (0, 0, 2), (2, 2, 3), (0, 3, 2), (0, 1, 2), (1, 2, 1), (1, 2, 2), (2, 2, 1), (2, 2,
    2))


def decode(code):
    code, hop = divmod(code, 4)
    code, direction = divmod(code, 2)
    code, index = divmod(code, 16)
    op, kind = divmod(code, 8)
    return op, (kind, index, direction, hop)


STEPS = tuple(tuple(decode(code) for code in group) for group in PROGRAM)
MESSAGES = tuple(sorted({m for group in STEPS for op, m in group if op == 1 and m[0] != XE}))
IDS = {m: n for n, m in enumerate(MESSAGES)}


def firsts(values):
    return tuple(min(n for n, v in enumerate(values) if v == value) for value in sorted(set(values)))


FRESH = firsts([b for _, _, b in ORDER])


def place(direction, hop):
    return hop if direction == 0 else (RING - hop) % RING


def split(value):
    high = value.astype(jnp.bfloat16)
    return high, (value - high.astype(jnp.float32)).astype(jnp.bfloat16)


def choose(t, values):
    chosen = jnp.int32(values[0])
    for number, value in enumerate(values[1:], 1):
        if value != values[number - 1]:
            chosen = jnp.where(t >= number, value, chosen)
    return chosen


def among(t, numbers):
    found = t == numbers[0]
    for number in numbers[1:]:
        found = jnp.logical_or(found, t == number)
    return found


def kernel(
    amp_hbm, int_hbm, a_hbm, v_hbm, out_ref, amp_ref, int_ref, am, vg, ag, ah, al, acc, rb, zs, zr, fin,
    isem, send, recv, lsem, xes, xer, r1s, r1r, r2s, r2r, r3s, r3r, ksem,
):
    row, col = lax.axis_index("row"), lax.axis_index("col")
    y, x = row // RING, row % RING
    z, k = col // 2, col % 2
    s = 1 - 2 * k
    first, second, depth = a_hbm.shape
    rows, width = v_hbm.shape
    pairs = first * second
    tiles = rows // TILE
    piece = (rows - CUT) // PARTS

    def device(dx=0, dy=0, dz=0, core=k):
        return (((y - s * dy + RING) % RING) * RING + (x - s * dx + RING) % RING, ((z - s * dz + SZ) % SZ) * 2 + core)

    sibling = device(core=1 - k)
    ahead, behind, across = device(dz=-1), device(dz=1), device(dz=-1, core=1 - k)

    loads = [
        pltpu.make_async_copy(source, target, isem.at[n])
        for n, (source, target) in enumerate(((int_hbm, int_ref), (v_hbm, vg.at[0, 0]), (amp_hbm, amp_ref), (a_hbm, am)))
    ]
    for load in loads:
        load.start()
    barrier = pltpu.get_barrier_semaphore()
    partners = [sibling, ahead, behind, across, device(dz=2), device(dz=-2)]
    partners += [device(dx=d) for d in (1, 2, 3)] + [device(dy=d) for d in (1, 3)]
    for partner in partners:
        pl.semaphore_signal(barrier, inc=1, device_id=partner, device_id_type=MESH)

    loads[0].wait()
    loads[1].wait()
    for r in range(tiles):
        for c in range(width // TILE):
            part = (0, 0, pl.ds(r * TILE, TILE), pl.ds(c * TILE, TILE))
            vg[part] = vg[part] * int_ref[c, col * tiles + r].astype(jnp.float32)

    loads[2].wait()
    loads[3].wait()

    @pl.loop(0, depth // TILE)
    def _(tile):
        part = pl.ds(pl.multiple_of(tile * TILE, TILE), TILE)
        for i in range(first):
            am[i, :, part] = am[i, :, part] * amp_ref[i, tile].astype(jnp.float32)

    pl.semaphore_wait(barrier, len(partners))

    def remote(source, target, send_sem, recv_sem, to):
        return pltpu.make_async_remote_copy(
            src_ref=source, dst_ref=target, send_sem=send_sem, recv_sem=recv_sem, device_id=to, device_id_type=MESH
        )

    def message(m):
        kind, index, direction, hop = m
        step = 1 if direction == 0 else -1
        here, there = place(direction, hop - 1), place(direction, hop)
        if kind == XA:
            block, foreign = index // 2, index % 2
            source, target, to = ag.at[block, here, foreign], ag.at[block, there, foreign], device(dx=-step)
        elif kind == B1:
            part = pl.ds(CUT + index * piece, piece)
            source, target, to = vg.at[0, here, part], vg.at[0, there, part], device(dz=-2 * step)
        elif kind == A1:
            part = pl.ds(0, CUT)
            source, target, to = vg.at[here, 0, part], vg.at[there, 0, part], device(dy=-step)
        elif kind == A2:
            part = pl.ds(0, CUT)
            source, target, to = vg.at[index, here, part], vg.at[index, there, part], device(dz=-2 * step)
        elif kind == B2:
            block, part = index // PARTS, pl.ds(CUT + index % PARTS * piece, piece)
            source, target, to = vg.at[here, block, part], vg.at[there, block, part], device(dy=-step)
        else:
            block, span = index // 2, pl.ds(*SPANS[1 + index % 2])
            rest = pl.ds(CUT, rows - CUT)
            source, target, to = vg.at[here, block, rest, span], vg.at[there, block, rest, span], device(dy=-step)
        return remote(source, target, send.at[IDS[m]], recv.at[IDS[m]], to)

    def columns(start, offset=0, size=None):
        return pl.ds(pl.multiple_of(start * width + offset, TILE), size or width)

    def block_of(owner, sense, core, j):
        return am.at[:, :, columns(2 * ((owner - sense * 2 * j + 2 * SZ) % SZ) + core)]

    def own(j):
        return pltpu.make_async_copy(block_of(z, s, k, j), ag.at[j, 0, 0, 0], lsem.at[j])

    def give(j, way):
        owner = z + s if way < 2 else z
        slot = ((1, 0), (1, 1), (0, 1))[way]
        sense, core = (s, k) if way == 0 else (-s, 1 - k)
        to = (ahead, across, sibling)[way]
        return remote(block_of(owner, sense, core, j), ag.at[(j, 0) + slot], xes.at[j, way], xer.at[j, way], to)

    def core_half(u, there):
        d, span = UNITS[u]
        span = pl.ds(*span)
        return remote(acc.at[d, :, :, 1, :, span], rb.at[UNITS[there][0], :, :, :, span], r1s.at[u], r1r.at[there], sibling)

    def z_half(u):
        d, span = UNITS[u]
        span = pl.ds(*span)
        return remote(zs.at[d, :, :, span], zr.at[d, :, :, span], r2s.at[u], r2r.at[u], behind)

    def home(u):
        d, span = UNITS[u]
        return columns((y - s * d + RING) % RING * RING + x, *span)

    def result(u, dx):
        d, span = UNITS[u]
        return remote(fin.at[d, dx, :, :, pl.ds(*span)], out_ref.at[:, :, home(u)], r3s.at[u, dx], r3r.at[u, dx], device(dx=dx))

    def kept(u):
        d, span = UNITS[u]
        return pltpu.make_async_copy(fin.at[d, 0, :, :, pl.ds(*span)], out_ref.at[:, :, home(u)], ksem.at[u])

    def stage(number, u):
        d, span = UNITS[u]
        block = (first, second, span[1])
        span = pl.ds(*span)
        if number == 0:
            core_half(u, (0, 2, 1, 3, 4)[u]).start()
        elif number == 1:
            core_half(u, u).wait_recv()
            for dx in range(RING):
                zs[d, dx, :, span] = acc[d, dx, 1, 0, :, span] + rb[d, (RING - dx) % RING, 1, :, span]
            for dx in range(RING):
                total = acc[d, dx, 0, 0, :, span] + rb[d, (RING - dx) % RING, 0, :, span]
                fin[d, dx, :, :, span] = total.reshape(block)
            z_half(u).start()
        else:
            z_half(u).wait_recv()
            for dx in (2, 1, 3, 0):
                total = fin[d, dx, :, :, span] + zr[d, dx, :, span].reshape(block)
                fin[d, dx, :, :, span] = total
            for dx in (2, 1, 3):
                result(u, dx).start()
            kept(u).start()

    def run(entry):
        op, m = entry
        if op == 2:
            stage(m[0], m[1])
        elif m[0] == XE:
            give(m[1], m[2]).start()
        elif op == 1:
            message(m).start()
        elif m[0] == LA:
            j = m[1] // 2
            if m[1] % 2:
                give(j, 0).wait_recv()
                give(j, 1).wait_recv()
            else:
                own(j).wait()
                give(j, 2).wait_recv()
        else:
            message(m).wait_recv()

    early = 0
    while STEPS[0][early][0] == 1:
        run(STEPS[0][early])
        early += 1
    for j in (0, 1, 3, 2):
        give(j, 2).start()
        own(j).start()
    for entry in STEPS[0][early:]:
        if entry[0] == 0 and entry[1][0] != LA:
            break
        run(entry)
        early += 1
    acc[...] = jnp.zeros_like(acc)
    for entry in STEPS[0][early:]:
        run(entry)

    @pl.loop(0, len(ORDER))
    def _(t):
        for number, group in enumerate(STEPS[:-1]):
            if group and number:

                @pl.when(t == number)
                def _():
                    for entry in group:
                        run(entry)

        dy, j = choose(t, [d for _, d, _ in ORDER]), choose(t, [b for _, _, b in ORDER])

        @pl.when(among(t, FRESH))
        def _():
            ah[j], al[j] = split(ag[j].reshape(ah.shape[1:]))

        for number, span in enumerate(SPANS):

            @pl.when(among(t, [n for n, (c, _, _) in enumerate(ORDER) if c == number]))
            def _():
                held = pl.ds(*span)
                high, low = split(vg[dy, j, :, held])
                product = jnp.dot(ah[j], high, preferred_element_type=jnp.float32)
                product += jnp.dot(ah[j], low, preferred_element_type=jnp.float32)
                product += jnp.dot(al[j], high, preferred_element_type=jnp.float32)
                acc[dy, :, :, :, :, held] += product.reshape(acc.shape[1:-1] + (span[1],))

    for entry in STEPS[-1]:
        run(entry)

    for u in range(len(UNITS)):
        core_half(u, u).wait_send()
        z_half(u).wait_send()
        for dx in (1, 2, 3):
            result(u, dx).wait()
        kept(u).wait()
    for j in range(RING):
        for way in (0, 1, 2):
            give(j, way).wait_send()
    for m in MESSAGES:
        message(m).wait_send()


def body(amplitudes, integrals, amp_pattern, int_pattern):
    first, second, depth = amplitudes.shape
    rows, width = integrals.shape
    pairs = first * second
    f32, bf16 = jnp.float32, jnp.bfloat16
    dma = pltpu.SemaphoreType.DMA
    units = len(UNITS)
    return pl.pallas_call(
        kernel,
        out_shape=pltpu.VMEM((first, second, depth), f32),
        in_specs=[pl.BlockSpec(memory_space=pl.ANY)] * 4,
        out_specs=pl.BlockSpec(memory_space=pl.ANY),
        scratch_shapes=[
            pltpu.SMEM(amp_pattern.shape, jnp.int32),
            pltpu.SMEM(int_pattern.shape[::-1], jnp.int32),
            pltpu.VMEM((first, second, depth), f32),
            pltpu.VMEM((RING, RING, rows, width), f32),
            pltpu.VMEM((RING, RING, 2, 2, first, second, width), f32),
            pltpu.VMEM((RING, RING * 4 * pairs, width), bf16),
            pltpu.VMEM((RING, RING * 4 * pairs, width), bf16),
            pltpu.VMEM((RING, RING, 2, 2, pairs, width), f32),
            pltpu.VMEM((RING, RING, 2, pairs, width), f32),
            pltpu.VMEM((RING, RING, pairs, width), f32),
            pltpu.VMEM((RING, RING, pairs, width), f32),
            pltpu.VMEM((RING, RING, first, second, width), f32),
            dma((4,)),
            dma((len(MESSAGES),)),
            dma((len(MESSAGES),)),
            dma((RING,)),
            dma((RING, 3)),
            dma((RING, 3)),
            dma((units,)),
            dma((units,)),
            dma((units,)),
            dma((units,)),
            dma((units, RING)),
            dma((units, RING)),
            dma((units,)),
        ],
        compiler_params=pltpu.CompilerParams(collective_id=0, has_side_effects=True, vmem_limit_bytes=46000 * 1024),
    )(*(pltpu.with_memory_space_constraint(o, pltpu.HBM) for o in (amp_pattern, int_pattern.T, amplitudes, integrals)))


def solution(mesh):
    placed = (P("col", "row", None), P("col", "row"), P("col", None), P(None, "row"))
    return jax.shard_map(
        body, mesh=mesh, in_specs=placed, out_specs=P("col", "row", None), check_vma=False
    )
```

profile of v0, /device:TPU:1, one launch (start us, length us, event | category | flops | bytes accessed | tf_op | source)
XLA Modules:
  0.0 101.8 jit_solution(292655531135979590)
XLA Ops:
  0.0 100.7 %shard_map.46 = f32[8,8,6144]{2,1,0:T(8,128)S(1)} custom-call(s32[8,48]{1,0:T(8,128)} %amp_hbm.1, s32[3,48]{1,0:T(4,128)} %bitcast.1, f32[8,8,6144]{2,1,0:T(8,128)} %a_hbm.1, f32[384,384]{1,0:T(8,128)} %v_hbm.1), custom_call_target="tpu_custom_call" | custom-call | tf_op jit(solution)/shard_map/pallas_call | solution.py:319
  100.7 1.1 %copy.6 = f32[8,8,6144]{2,1,0:T(8,128)} copy(f32[8,8,6144]{2,1,0:T(8,128)S(1)} %shard_map.46) | data formatting | bytes 3145728
where the time goes:
time: 102 us
  Pallas kernels  101 us (99%)
  local copies, waits for them, and re-layouts  1.15 us (1%)
    pallas_call x1, Pallas kernels, body(): pl.pallas_call(kernel, out_shape=pltpu.VMEM((first, second, depth), f32),...  101 us

commit v1 on v0

--- a/solution.py
+++ b/solution.py
@@ -13,37 +13,60 @@
 CUT = 32
 FULL, WIDE, NARROW = (0, 384), (0, 256), (256, 128)
 SPANS = (FULL, WIDE, NARROW)
-UNITS = ((0, FULL), (1, FULL), (3, FULL), (2, WIDE), (2, NARROW))
+UNITS = ((0, (0, 384)), (1, (0, 384)), (3, (0, 384)), (2, (0, 256)), (2, (256, 128)))
+MIRROR = tuple(UNITS.index(((RING - d) % RING, span)) for d, span in UNITS)
 
 PROGRAM = (
-    (1153, 1793, 1157, 1797, 1664, 1668, 1029, 1037, 512, 1409, 1413, 528, 1425, 1429, 1025, 1672, 560, 1457, 1461,
-     1161, 1165, 769, 1794, 520, 1417, 1421, 1925, 5, 1201, 1205, 385, 1410, 544, 1445, 129, 137, 1282, 1676, 1,
-     1173, 1688, 401, 1426, 1169, 1692, 536, 1437, 1680, 393, 1418, 1933, 1684, 13, 1213, 773, 1949, 568, 1469,
-     1033, 1209, 1433, 770, 1941, 1026, 552, 1453, 1465, 1290, 386, 389, 394, 397,),
-    (),
-    (433, 1458, 177, 185, 1330, 1921, 133, 141,),
-    (409, 1434, 9, 1177, 1181, 258,),
-    (266,),
-    (441, 1466, 1441, 1034, 1338, 1929, 2, 1189, 1449, 897, 402, 405, 410, 413,),
-    (901, 434, 437, 442, 445,),
-    (417, 1442, 909,),
-    (1185, 1922, 1945, 181, 189, 925,),
-    (425, 1450, 10, 1193, 1197, 905, 1930, 145, 153,),
-    (1937, 306, 917,),
+    (1153, 1161, 1157, 1165, 1664, 1668, 1029, 1037, 512, 1409, 1413, 528, 1425, 1429, 1025, 1672, 560, 1457, 1461,
+     1793, 1797, 520, 1417, 1421, 1925, 5, 1201, 129, 137, 1282, 1205, 385, 1410, 544, 1445, 1676, 1, 1173, 1688,
+     401, 1426, 1169, 1692, 536, 1437, 1033, 393, 1418, 769, 1933, 386, 389,),
+    (13, 1213, 1026,),
+    (568, 1469, 773, 1949, 133, 141,),
+    (1433, 1794, 1465, 1209, 1290, 394, 397,),
+    (433, 1458, 1680, 770, 1941,),
+    (9, 1181,),
+    (409, 1434, 1177, 258,),
+    (),
+    (441, 1466, 177, 185, 1330, 901, 434, 437,),
+    (1441, 1684, 909,),
+    (1034, 181, 189, 925,),
+    (2, 1189, 1921, 266,),
+    (),
+    (1185, 552, 1449, 1453, 442, 445,),
+    (),
+    (),
+    (417, 1442, 1929, 1945, 10, 1197, 1193, 1937, 425, 1450, 897, 410, 413,),
+    (1922, 402, 405,),
+    (905, 1930, 145, 153,),
     (921, 1946, 149, 157,),
-    (913, 1938, 898, 418, 421, 426, 429,),
-    (2048, 1298, 314,),
-    (165, 173, 922,),
-    (2064, 2176, 161, 169, 1314, 906,),
-    (2056, 1306, 2184, 274,),
-    (2192, 2304, 1322, 290, 914,),
-    (2072, 2312, 282,),
-    (2200, 298,),
-    (2080, 2320, 2208, 2328, 2336,),
+    (913, 1938,),
+    (898, 426, 429,),
+    (2048, 1298, 418, 421,),
+    (2304, 165, 173, 922,),
+    (2064, 2176, 1306,),
+    (),
+    (2320, 161, 169, 906,),
+    (2056, 2184,),
+    (2312, 1314, 306, 917,),
+    (2192, 274,),
+    (2432, 1338,),
+    (),
+    (282,),
+    (),
+    (1322, 2440, 290, 914,),
+    (2072,),
+    (2328, 314,),
+    (2200,),
+    (2448, 298,),
+    (2080,),
+    (2336, 2208, 2456, 2464,),
 )
-ORDER = ((0, 0, 0), (0, 1, 0), (0, 3, 0), (1, 2, 0), (2, 2, 0), (0, 0, 1), (0, 0, 3), (0, 1, 3), (0, 3, 3), (0, 1,
-    1), (1, 2, 3), (0, 3, 1), (0, 0, 2), (2, 2, 3), (0, 3, 2), (0, 1, 2), (1, 2, 1), (1, 2, 2), (2, 2, 1), (2, 2,
-    2))
+ORDER = ((0, 0, 0, 0), (0, 1, 0, 0), (0, 3, 0, 0), (0, 0, 0, 1), (0, 1, 0, 1), (0, 3, 0, 1), (1, 2, 0, 1), (1, 2, 0,
+    0), (0, 0, 3, 0), (0, 1, 3, 0), (0, 3, 3, 0), (2, 2, 0, 1), (2, 2, 0, 0), (0, 0, 3, 1), (0, 1, 3, 1), (0, 3, 3,
+    1), (0, 0, 1, 1), (0, 0, 1, 0), (0, 1, 1, 1), (0, 3, 1, 1), (0, 1, 1, 0), (0, 0, 2, 1), (0, 0, 2, 0), (0, 3, 2,
+    1), (0, 3, 1, 0), (0, 3, 2, 0), (0, 1, 2, 1), (0, 1, 2, 0), (1, 2, 3, 1), (1, 2, 1, 1), (1, 2, 1, 0), (1, 2, 3,
+    0), (2, 2, 1, 1), (2, 2, 1, 0), (1, 2, 2, 1), (1, 2, 2, 0), (2, 2, 3, 1), (2, 2, 3, 0), (2, 2, 2, 1), (2, 2, 2,
+    0))
 
 
 def decode(code):
@@ -63,7 +86,7 @@
     return tuple(min(n for n, v in enumerate(values) if v == value) for value in sorted(set(values)))
 
 
-FRESH = firsts([b for _, _, b in ORDER])
+FRESH = firsts([b * 2 + a for _, _, b, a in ORDER])
 
 
 def place(direction, hop):
@@ -76,18 +99,22 @@
 
 
 def choose(t, values):
-    chosen = jnp.int32(values[0])
-    for number, value in enumerate(values[1:], 1):
-        if value != values[number - 1]:
-            chosen = jnp.where(t >= number, value, chosen)
-    return chosen
-
-
-def among(t, numbers):
-    found = t == numbers[0]
-    for number in numbers[1:]:
-        found = jnp.logical_or(found, t == number)
-    return found
+    words = [sum(v << (2 * n) for n, v in enumerate(values[w : w + 15])) for w in range(0, len(values), 15)]
+    word = jnp.int32(words[0])
+    for number, value in enumerate(words[1:], 1):
+        word = jnp.where(t >= 15 * number, value, word)
+    return lax.shift_right_logical(word, 2 * (t % 15)) & 3
+
+
+def at_step(t, actions, width=7):
+    for low in range(0, len(actions), width):
+        group = [(n, act) for n, act in enumerate(actions[low : low + width], low) if act]
+        if group:
+
+            @pl.when(jnp.logical_and(t >= low, t < low + width))
+            def _():
+                for number, act in group:
+                    pl.when(t == number)(act)
 
 
 def kernel(
@@ -186,10 +213,16 @@
         to = (ahead, across, sibling)[way]
         return remote(block_of(owner, sense, core, j), ag.at[(j, 0) + slot], xes.at[j, way], xer.at[j, way], to)
 
-    def core_half(u, there):
+    def core_half(u, foreign, there):
         d, span = UNITS[u]
         span = pl.ds(*span)
-        return remote(acc.at[d, :, :, 1, :, span], rb.at[UNITS[there][0], :, :, :, span], r1s.at[u], r1r.at[there], sibling)
+        return remote(
+            acc.at[d, foreign, :, 1, :, span],
+            rb.at[UNITS[there][0], foreign, :, :, span],
+            r1s.at[u, foreign],
+            r1r.at[there, foreign],
+            sibling,
+        )
 
     def z_half(u):
         d, span = UNITS[u]
@@ -212,21 +245,19 @@
         d, span = UNITS[u]
         block = (first, second, span[1])
         span = pl.ds(*span)
-        if number == 0:
-            core_half(u, (0, 2, 1, 3, 4)[u]).start()
+        if number % 2 == 0:
+            core_half(u, 1 - number // 2, MIRROR[u]).start()
         elif number == 1:
-            core_half(u, u).wait_recv()
+            core_half(u, 1, u).wait_recv()
             for dx in range(RING):
-                zs[d, dx, :, span] = acc[d, dx, 1, 0, :, span] + rb[d, (RING - dx) % RING, 1, :, span]
-            for dx in range(RING):
-                total = acc[d, dx, 0, 0, :, span] + rb[d, (RING - dx) % RING, 0, :, span]
-                fin[d, dx, :, :, span] = total.reshape(block)
+                zs[d, dx, :, span] = acc[d, 1, dx, 0, :, span] + rb[d, 1, (RING - dx) % RING, :, span]
             z_half(u).start()
         else:
+            core_half(u, 0, u).wait_recv()
             z_half(u).wait_recv()
             for dx in (2, 1, 3, 0):
-                total = fin[d, dx, :, :, span] + zr[d, dx, :, span].reshape(block)
-                fin[d, dx, :, :, span] = total
+                total = acc[d, 0, dx, 0, :, span] + rb[d, 0, (RING - dx) % RING, :, span] + zr[d, dx, :, span]
+                fin[d, dx, :, :, span] = total.reshape(block)
             for dx in (2, 1, 3):
                 result(u, dx).start()
             kept(u).start()
@@ -268,36 +299,39 @@
 
     @pl.loop(0, len(ORDER))
     def _(t):
-        for number, group in enumerate(STEPS[:-1]):
-            if group and number:
-
-                @pl.when(t == number)
-                def _():
-                    for entry in group:
-                        run(entry)
-
-        dy, j = choose(t, [d for _, d, _ in ORDER]), choose(t, [b for _, _, b in ORDER])
-
-        @pl.when(among(t, FRESH))
+        def events(group):
+            def act():
+                for entry in group:
+                    run(entry)
+
+            return act
+
+        at_step(t, [events(group) if group and number else None for number, group in enumerate(STEPS[:-1])])
+        dy, j, foreign = (choose(t, [entry[n] for entry in ORDER]) for n in (1, 2, 3))
+
+        @pl.when(choose(t, [int(n in FRESH) for n in range(len(ORDER))]) == 1)
         def _():
-            ah[j], al[j] = split(ag[j].reshape(ah.shape[1:]))
-
+            value = ag[j, :, foreign]
+            ah[j, foreign], al[j, foreign] = split(value.reshape(ah.shape[2:]))
+
+        columns_of = choose(t, [entry[0] for entry in ORDER])
         for number, span in enumerate(SPANS):
 
-            @pl.when(among(t, [n for n, (c, _, _) in enumerate(ORDER) if c == number]))
+            @pl.when(columns_of == number)
             def _():
                 held = pl.ds(*span)
                 high, low = split(vg[dy, j, :, held])
-                product = jnp.dot(ah[j], high, preferred_element_type=jnp.float32)
-                product += jnp.dot(ah[j], low, preferred_element_type=jnp.float32)
-                product += jnp.dot(al[j], high, preferred_element_type=jnp.float32)
-                acc[dy, :, :, :, :, held] += product.reshape(acc.shape[1:-1] + (span[1],))
+                product = jnp.dot(ah[j, foreign], high, preferred_element_type=jnp.float32)
+                product += jnp.dot(ah[j, foreign], low, preferred_element_type=jnp.float32)
+                product += jnp.dot(al[j, foreign], high, preferred_element_type=jnp.float32)
+                acc[dy, foreign, :, :, :, held] += product.reshape(acc.shape[2:-1] + (span[1],))
 
     for entry in STEPS[-1]:
         run(entry)
 
     for u in range(len(UNITS)):
-        core_half(u, u).wait_send()
+        core_half(u, 0, u).wait_send()
+        core_half(u, 1, u).wait_send()
         z_half(u).wait_send()
         for dx in (1, 2, 3):
             result(u, dx).wait()
@@ -327,10 +361,10 @@
             pltpu.VMEM((first, second, depth), f32),
             pltpu.VMEM((RING, RING, rows, width), f32),
             pltpu.VMEM((RING, RING, 2, 2, first, second, width), f32),
-            pltpu.VMEM((RING, RING * 4 * pairs, width), bf16),
-            pltpu.VMEM((RING, RING * 4 * pairs, width), bf16),
-            pltpu.VMEM((RING, RING, 2, 2, pairs, width), f32),
-            pltpu.VMEM((RING, RING, 2, pairs, width), f32),
+            pltpu.VMEM((RING, 2, RING * 2 * pairs, width), bf16),
+            pltpu.VMEM((RING, 2, RING * 2 * pairs, width), bf16),
+            pltpu.VMEM((RING, 2, RING, 2, pairs, width), f32),
+            pltpu.VMEM((RING, 2, RING, pairs, width), f32),
             pltpu.VMEM((RING, RING, pairs, width), f32),
             pltpu.VMEM((RING, RING, pairs, width), f32),
             pltpu.VMEM((RING, RING, first, second, width), f32),
@@ -340,8 +374,8 @@
             dma((RING,)),
             dma((RING, 3)),
             dma((RING, 3)),
-            dma((units,)),
-            dma((units,)),
+            dma((units, 2)),
+            dma((units, 2)),
             dma((units,)),
             dma((units,)),
             dma((units, RING)),

time: 102 us -> 101 us (level)
  Pallas kernels: 101 us -> 99.8 us
where the time goes in v1:
time: 101 us
  Pallas kernels  99.8 us (99%)
  local copies, waits for them, and re-layouts  1.15 us (1%)
    pallas_call x1, Pallas kernels, body(): pl.pallas_call(kernel, out_shape=pltpu.VMEM((first, second, depth), f32),...  99.8 us

profile of v1, /device:TPU:1, one launch (start us, length us, event | category | flops | bytes accessed | tf_op | source)
XLA Modules:
  0.0 101.0 jit_solution(8910371902577946498)
XLA Ops:
  0.0 99.8 %shard_map.46 = f32[8,8,6144]{2,1,0:T(8,128)S(1)} custom-call(s32[8,48]{1,0:T(8,128)} %amp_hbm.1, s32[3,48]{1,0:T(4,128)} %bitcast.1, f32[8,8,6144]{2,1,0:T(8,128)} %a_hbm.1, f32[384,384]{1,0:T(8,128)} %v_hbm.1), custom_call_target="tpu_custom_call" | custom-call | tf_op jit(solution)/shard_map/pallas_call | solution.py:353
  99.8 1.1 %copy.6 = f32[8,8,6144]{2,1,0:T(8,128)} copy(f32[8,8,6144]{2,1,0:T(8,128)S(1)} %shard_map.46) | data formatting | bytes 3145728

commit v2 on v1

--- a/solution.py
+++ b/solution.py
@@ -321,9 +321,8 @@
             def _():
                 held = pl.ds(*span)
                 high, low = split(vg[dy, j, :, held])
-                product = jnp.dot(ah[j, foreign], high, preferred_element_type=jnp.float32)
-                product += jnp.dot(ah[j, foreign], low, preferred_element_type=jnp.float32)
-                product += jnp.dot(al[j, foreign], high, preferred_element_type=jnp.float32)
+                left = jnp.concatenate([ah[j, foreign], al[j, foreign], ah[j, foreign]], axis=1)
+                product = jnp.dot(left, jnp.concatenate([high, high, low], axis=0), preferred_element_type=jnp.float32)
                 acc[dy, foreign, :, :, :, held] += product.reshape(acc.shape[2:-1] + (span[1],))
 
     for entry in STEPS[-1]:

time: 101 us -> 101 us (level)
  no operation moved by 1% of the time
where the time goes in v2:
time: 101 us
  Pallas kernels  99.5 us (99%)
  local copies, waits for them, and re-layouts  1.15 us (1%)
    pallas_call x1, Pallas kernels, body(): pl.pallas_call(kernel, out_shape=pltpu.VMEM((first, second, depth), f32),...  99.5 us

profile of v2, /device:TPU:1, one launch (start us, length us, event | category | flops | bytes accessed | tf_op | source)
XLA Modules:
  0.0 100.6 jit_solution(4957902799012603142)
XLA Ops:
  0.0 99.5 %shard_map.46 = f32[8,8,6144]{2,1,0:T(8,128)S(1)} custom-call(s32[8,48]{1,0:T(8,128)} %amp_hbm.1, s32[3,48]{1,0:T(4,128)} %bitcast.1, f32[8,8,6144]{2,1,0:T(8,128)} %a_hbm.1, f32[384,384]{1,0:T(8,128)} %v_hbm.1), custom_call_target="tpu_custom_call" | custom-call | tf_op jit(solution)/shard_map/pallas_call | solution.py:352
  99.5 1.1 %copy.6 = f32[8,8,6144]{2,1,0:T(8,128)} copy(f32[8,8,6144]{2,1,0:T(8,128)S(1)} %shard_map.46) | data formatting | bytes 3145728
